TPU v7x, 128 devices: a whole 4x4x4 slice. The times are simulated.
128 devices in a mesh: chan: 16 (over y, z), win: 8 (over x, core).
Axes of the slice: x: 4, y: 4, z: 4, core: 2. Of those that a mesh axis runs over, the one named last changes fastest.
Arguments:
- spectra: bfloat16 [768, 32, 2, 1024], P('chan', 'win'), may hold values from -120 to 120
- sources: int32 [4], replicated, may hold values from 0 to 767
- bin_rows: int32 [4, 16, 32, 3], P(None, 'chan'), may hold values from -1 to 47, as said below
Outputs:
- stacked: float32 [4, 32, 4096], P(None, 'chan', 'win')
Inputs may be any that keep to these rules, and one draw needn't show every extreme that they name: `bin_rows`: for every step and every index d of chan, the entries name each of that device's 48 local receiver rows exactly once; within a bin the used slots come first and the rest are -1. In each step one bin uses all 3 slots on every device.
All inputs are finite; a program needn't handle non-finite values.
Results may differ from a plain program's by a relative error of at most 0.0099.
Values may be sent and summed in bfloat16 or wider, within the bound.
No kernel may reach another device: no remote copies, remote signals or barrier semaphores. Data moves between devices by JAX's collectives and lax.ppermute only.
A program may use at most 768 MiB of HBM per device.

v0:
```python
import jax
import jax.numpy as jnp
from jax import lax
from jax.sharding import PartitionSpec as P

F = 1024
F0 = 32
NFFT = 8192
LMAX = 2048
HW = 32
NBINS = 32
MOST = 3
LAGS = 4096
epsilon_amp = 1e-06
phase_floor = 0.1


def broadcast(block, axis, source):
    block = jnp.where(lax.axis_index(axis) == source, block, jnp.zeros_like(block))
    return lax.psum(block, axis)


def band_matrix():
    index = jnp.arange(F, dtype=jnp.int32)
    inside = jnp.abs(index[:, None] - index[None, :]) <= HW
    return inside.astype(jnp.float32) / (2 * HW + 1)


def whiten(spectra):
    real_part = spectra[:, :, 0, :].astype(jnp.float32)
    imag_part = spectra[:, :, 1, :].astype(jnp.float32)
    amplitude = jnp.sqrt(real_part * real_part + imag_part * imag_part)
    smooth = jnp.dot(amplitude.reshape(-1, F), band_matrix(), precision=lax.Precision.HIGHEST)
    smooth = smooth.reshape(amplitude.shape) + epsilon_amp
    return jnp.stack([real_part / smooth, imag_part / smooth], axis=2).astype(jnp.bfloat16)


def cross_spectra(white, source):
    white_real = white[..., 0, :].astype(jnp.float32)
    white_imag = white[..., 1, :].astype(jnp.float32)
    source_real = source[..., 0, :].astype(jnp.float32)
    source_imag = source[..., 1, :].astype(jnp.float32)
    cross_real = white_real * source_real + white_imag * source_imag
    cross_imag = white_imag * source_real - white_real * source_imag
    return jnp.concatenate([cross_real, cross_imag], axis=-1).astype(jnp.bfloat16)


def lag_table(first_lag, lag_count):
    frequency = F0 + jnp.arange(F, dtype=jnp.int32)
    lag_index = first_lag + jnp.arange(lag_count, dtype=jnp.int32) - LMAX
    turn_count = jnp.mod(frequency[:, None] * lag_index[None, :], NFFT)
    angle_rad = turn_count.astype(jnp.float32) * (2.0 * jnp.pi / NFFT)
    cosine = jnp.cos(angle_rad)
    sine_part = jnp.sin(angle_rad)
    upper_half = jnp.concatenate([cosine, sine_part], axis=1)
    lower_half = jnp.concatenate([-sine_part, cosine], axis=1)
    return jnp.concatenate([upper_half, lower_half], axis=0).astype(jnp.bfloat16)


def correlate_block(cross_rows, first_lag, lag_count, windows):
    analytic = jnp.dot(
        cross_rows, lag_table(first_lag, lag_count), preferred_element_type=jnp.float32
    )
    analytic = analytic * (1.0 / jnp.sqrt(jnp.float32(F)))
    real_part = analytic[:, :lag_count]
    imag_part = analytic[:, lag_count:]
    magnitude = jnp.maximum(jnp.sqrt(real_part * real_part + imag_part * imag_part), phase_floor)
    terms = jnp.stack([real_part, real_part / magnitude, imag_part / magnitude], axis=1)
    return terms.reshape(-1, windows, 3, lag_count).sum(axis=1)


def weigh_stack(totals, counts, windows):
    traces = jnp.maximum(counts, 1.0) * windows
    linear = totals[..., 0, :]
    power = totals[..., 1, :] * totals[..., 1, :] + totals[..., 2, :] * totals[..., 2, :]
    return linear / jnp.sqrt(traces)[..., None] * power / traces[..., None]


def gather_rows(partial_value, slot_rows, chan_count):
    is_live = slot_rows >= 0
    safe_rows = jnp.maximum(slot_rows, 0)
    picked = jax.vmap(lambda block_rows, chosen: block_rows[chosen])(partial_value, safe_rows)
    picked = picked * is_live[..., None, None].astype(jnp.float32)
    step_count = slot_rows.shape[0]
    slot_count = NBINS * MOST // chan_count
    buffer = picked.reshape(step_count, chan_count, slot_count, 3, partial_value.shape[-1])
    live_mask = is_live.astype(jnp.float32).reshape(step_count, chan_count, slot_count)
    return (buffer, live_mask)


def fold_slots(received, live_mask):
    step_count, chan_count, slot_count = live_mask.shape
    bin_count = slot_count // MOST
    totals = received.reshape(step_count, chan_count, bin_count, MOST, 3, received.shape[-1]).sum(
        axis=(1, 3)
    )
    counts = live_mask.reshape(step_count, chan_count, bin_count, MOST).sum(axis=(1, 3))
    return (totals, counts)


def shards(spectra, sources, bin_rows):
    chan_dev = spectra.shape[0]
    win_dev = spectra.shape[1]
    chan_count = lax.axis_size("chan")
    windows = win_dev * lax.axis_size("win")
    step_count = sources.shape[0]
    white = whiten(spectra)
    owners = sources // chan_dev
    local_rows = sources % chan_dev
    gathered = []
    for step_index in range(step_count):
        own_row = lax.dynamic_index_in_dim(white, local_rows[step_index], 0, keepdims=False)
        gathered.append(broadcast(own_row, "chan", owners[step_index]))
    source = jnp.stack(gathered)
    cross_rows = cross_spectra(white[None], source[:, None]).reshape(-1, 2 * F)
    block_len = min(256, LAGS)
    block_count = LAGS // block_len

    def one_block(block):
        return correlate_block(cross_rows, block * block_len, block_len, win_dev)

    pieces = lax.map(one_block, jnp.arange(block_count, dtype=jnp.int32))
    pieces = pieces.reshape(block_count, step_count, chan_dev, 3, block_len)
    partial_value = jnp.transpose(pieces, (1, 2, 3, 0, 4)).reshape(step_count, chan_dev, 3, LAGS)
    slot_rows = bin_rows[:, 0]
    buffer, live_mask = gather_rows(partial_value, slot_rows, chan_count)
    received, live_got = (
        lax.all_to_all(buffer, "chan", split_axis=1, concat_axis=1, tiled=True),
        lax.all_to_all(live_mask, "chan", split_axis=1, concat_axis=1, tiled=True),
    )
    totals, counts = fold_slots(received, live_got)
    totals = lax.psum_scatter(totals, "win", scatter_dimension=3, tiled=True)
    return weigh_stack(totals, counts, windows)


def solution(mesh):
    in_specs = (P("chan", "win", None, None), P(), P(None, "chan", None, None))
    out_specs = P(None, "chan", "win")
    return jax.shard_map(shards, mesh=mesh, in_specs=in_specs, out_specs=out_specs, check_vma=False)
```

profile of v0, /device:TPU:0, one launch (start us, length us, event | category | flops | bytes accessed | tf_op | source)
XLA Modules:
  0.0 759.1 jit_solution(268665359414033061)
XLA Ops:
  15.4 3.4 fusion.45
  21.3 4.2 fusion.30
  29.7 82.3 %all-reduce.3.cloned.1.call-done = (bf16[1,4,2,1024]{3,0,1,2:T(2,128)(2,1)}, bf16[1,4,2,1024]{3,0,1,2:T(2,128)(2,1)}, bf16[1,4,2,1024]{3,0,1,2:T(2,128)(2,1)}, bf16[1,4,2,1024]{3,0,1,2:T(2,128)(2,1)}) async-done(((bf16[1,4,2,1024]{3,0,1,2:T(2,128)(2,1)}, bf16[1,4,2,1024]{3,0,1,2:T(2,128)(2,1)}, bf16[1,4,2,1024]{3,0,1,2:T(2,128)(2,1)}, bf16[1,4,2,1024]{3,0,1,2:T(2,128)(2,1)}), ...) | async-done | bytes 65552 | tf_op jit(solution)/shard_map/psum | solution.py:20
  113.1 2.8 add_convert_fusion
  115.9 1.9 add.117
  117.8 1.9 sub.32
  119.6 3.4 pad_maximum_fusion
  123.0 227.3 %while.12 = (s32[]{:T(128)}, f32[16,192,3,256]{3,1,2,0:T(8,128)}, s32[16]{0:T(128)S(1)}, bf16[768,2048]{1,0:T(8,128)(2,1)}, s32[]{:T(128)}, /*index=5*/s32[1]{0:T(128)}) while((s32[]{:T(128)}, f32[16,192,3,256]{3,1,2,0:T(8,128)}, s32[16]{0:T(128)S(1)}, bf16[768,2048]{1,0:T(8,128)(2,1)}, s32[]{:T(128)}, /*index=5*/s32[1]{0:T(128)}) %tuple.55), condition=%wide.region_6.7_spmd, body=%wide.region_4.6_spmd.sunk | while | flops 1626916352 | bytes 25373280 | solution.py:122
  124.3 4.7 fusion.55
  129.1 3.7 multiply_bitcast_fusion.2
  134.7 1.6 maximum_reduce_fusion.2
  138.5 4.7 fusion.55
  143.2 3.7 multiply_bitcast_fusion.2
  148.8 1.6 maximum_reduce_fusion.2
  152.6 4.7 fusion.55
  157.4 3.7 multiply_bitcast_fusion.2
  163.0 1.6 maximum_reduce_fusion.2
  166.9 4.7 fusion.55
  171.6 3.7 multiply_bitcast_fusion.2
  177.2 1.6 maximum_reduce_fusion.2
  181.0 4.7 fusion.55
  185.8 3.7 multiply_bitcast_fusion.2
  191.4 1.6 maximum_reduce_fusion.2
  195.2 4.7 fusion.55
  199.9 3.7 multiply_bitcast_fusion.2
  205.6 1.6 maximum_reduce_fusion.2
  209.4 4.7 fusion.55
  214.1 3.7 multiply_bitcast_fusion.2
  219.7 1.6 maximum_reduce_fusion.2
  223.5 4.7 fusion.55
  228.3 3.7 multiply_bitcast_fusion.2
  233.9 1.6 maximum_reduce_fusion.2
  237.7 4.7 fusion.55
  242.4 3.7 multiply_bitcast_fusion.2
  248.0 1.6 maximum_reduce_fusion.2
  251.9 4.7 fusion.55
  256.6 3.7 multiply_bitcast_fusion.2
  262.2 1.6 maximum_reduce_fusion.2
  266.1 4.7 fusion.55
  270.8 3.7 multiply_bitcast_fusion.2
  280.2 4.7 fusion.55
  284.9 3.7 multiply_bitcast_fusion.2
  294.4 4.7 fusion.55
  299.1 3.7 multiply_bitcast_fusion.2
  308.6 4.7 fusion.55
  313.3 3.7 multiply_bitcast_fusion.2
  322.7 4.7 fusion.55
  327.4 3.7 multiply_bitcast_fusion.2
  336.9 4.7 fusion.55
  341.7 3.7 multiply_bitcast_fusion.2
  350.4 13.8 %copy.118 = f32[16,4,48,3,256]{4,0,2,3,1:T(8,128)} copy(f32[16,4,48,3,256]{4,2,1,3,0:T(8,128)} %bitcast.98) | data formatting | bytes 18874368 | tf_op jit(solution)/shard_map/reshape | solution.py:123
  364.2 11.3 %reshape.190 = f32[4,48,3,4096]{3,1,2,0:T(8,128)} reshape(f32[4,48,3,16,256]{4,3,1,2,0:T(8,128)} %bitcast.96) | data formatting | bytes 18874368 | tf_op jit(solution)/shard_map/reshape | solution.py:124
  375.5 14.8 %copy.82 = f32[4,48,3,4096]{3,2,1,0:T(4,128)} copy(f32[4,48,3,4096]{3,1,2,0:T(8,128)} %reshape.190) | data formatting | bytes 18874368 | tf_op jit(solution)/shard_map/reshape | solution.py:124
  390.3 31.4 %gather_fusion = f32[384,3,4096]{2,1,0:T(4,128)} fusion(f32[4,48,3,4096]{3,2,1,0:T(4,128)} %copy.82, s32[384]{0:T(512)S(1)} %reshape.200), kind=kCustom, calls=%fused_computation | custom fusion | bytes 37751808 | tf_op jit(solution)/shard_map/vmap()/gather | solution.py:82
  421.7 12.7 %copy_multiply_fusion = f32[4,16,6,3,4096]{4,2,1,0,3:T(8,128)S(1)} fusion(f32[4,16,6,3,4096]{4,3,2,1,0:T(4,128)} %bitcast.95, f32[4,16,6]{2,1,0:T(8,128)S(1)} %reshape.199), kind=kLoop, calls=%fused_computation.30 | loop fusion | flops 4718592 | bytes 37750272 | tf_op jit(solution)/shard_map/mul | solution.py:83
  434.4 17.2 %copy.85 = f32[4,16,6,3,4096]{4,0,3,2,1:T(4,128)} copy(f32[4,16,6,3,4096]{4,2,1,0,3:T(8,128)S(1)} %copy_multiply_fusion) | data formatting | bytes 37748736 | tf_op jit(solution)/shard_map/mul | solution.py:83
  451.7 213.3 %all_to_all.10 = f32[4,16,6,3,4096]{4,0,3,2,1:T(4,128)} all-to-all(f32[4,16,6,3,4096]{4,0,3,2,1:T(4,128)} %copy.85), channel_id=1, replica_groups=mesh['chan'=16,'win'=8] {'chan'}, dimensions={1} | all-to-all | bytes 37748736 | tf_op jit(solution)/shard_map/all_to_all | solution.py:128
  665.0 10.5 %reduce_sum.44 = f32[4,6,3,4096]{3,0,2,1:T(4,128)S(1)} reduce(f32[4,16,6,3,4096]{4,0,3,2,1:T(4,128)} %all_to_all.10, f32[]{:T(128)} %constant.115.clone.1), dimensions={1}, to_apply=%region_7.8 | reduce | flops 4423680 | bytes 20054020 | tf_op jit(solution)/shard_map/reduce_sum | solution.py:94
  675.8 16.9 %copy.91 = f32[4,2,3,4096]{1,0,2,3:T(4,128)} copy(f32[4,2,3,4096]{3,0,2,1:T(4,128)S(1)} %reduce_sum.46) | data formatting | bytes 786432
  692.7 18.1 %reshape.213 = f32[4096,24]{1,0:T(8,128)} reshape(f32[4096,3,4,2]{3,2,1,0:T(4,128)} %bitcast.94) | data formatting | bytes 786432
  710.8 11.1 %all_to_all.11 = f32[4,16,6]{2,0,1:T(4,128)S(1)} all-to-all(f32[4,16,6]{2,0,1:T(4,128)S(1)} %copy.89), channel_id=1, replica_groups=mesh['chan'=16,'win'=8] {'chan'}, dimensions={1} | all-to-all | bytes 3072 | tf_op jit(solution)/shard_map/all_to_all | solution.py:129
  722.1 20.2 %reduce-scatter.4.cloned.1.call-done = f32[512,24]{1,0:T(8,128)} async-done(((f32[4096,24]{1,0:T(8,128)}), f32[512,24]{1,0:T(8,128)}) %reduce-scatter.4.cloned.1.call-update) | async-done | bytes 49168
  742.3 2.5 reshape.214
  744.8 1.9 fusion.44
  (217 shorter events, 76.3 us)
Async XLA Ops:
  6.5 105.5 %all-reduce.3.cloned.1.call-start = ((), (), s32[]{:S(2)}) async-start(), calls=%async_computation.4 | async-start | bytes 262144 | tf_op jit(solution)/shard_map/psum | solution.py:20
  21.3 5.4 copy-start.1
  26.4 716.0 %reduce-scatter.4.cloned.1.call-start = ((), (), s32[]{:S(2)}) async-start(), calls=%async_computation.3 | async-start | bytes 2359296
  117.8 1.9 copy-start
Sparse Core Ops, SparseCore 0:
  26.5 85.4 all-reduce.2
  710.9 31.3 reduce-scatter.3
where the time goes:
time: 766 us; the launch traced here: 759 us
  blocking collectives  224 us (29%)
  local copies, waits for them, and re-layouts  191 us (25%)
  other arithmetic  141 us (18%)
  waiting for transfers between devices  103 us (13%)
  matrix products  63.9 us (8%)
  between operations  23.8 us (3%)
  loops' own time  11.9 us (2%)
    all_to_all x1, blocking collectives, shards(): lax.all_to_all(buffer, 'chan', split_axis=1, concat_axis=1, tiled=True)  213 us
    psum x1, waiting for transfers between devices, broadcast(): return lax.psum(block, axis)  82.3 us
    another operation x17, other arithmetic  78.3 us
    dot_general x16, matrix products, correlate_block(): jnp.dot(cross_rows, lag_table(first_lag, lag_count), preferred_element_ty...  59.6 us
    unnamed x10, local copies, waits for them, and re-layouts  42.2 us
    gather x3, local copies, waits for them, and re-layouts, gather_rows(): block_rows[chosen]  31.7 us
    reduce_sum x16, other arithmetic, correlate_block(): return terms.reshape(-1, windows, 3, lag_count).sum(axis=1)  26.3 us
    reshape x2, local copies, waits for them, and re-layouts, shards(): jnp.transpose(pieces, (1, 2, 3, 0, 4))  26.1 us
  transfers between devices with their start and end apart: 2, of which 2 were waited for; matrix products, arithmetic and copies ran while one was open for 0% of the time, Pallas kernels for 0%

commit v1 on v0

--- a/solution.py
+++ b/solution.py
@@ -17,7 +17,7 @@
 
 def broadcast(block, axis, source):
     block = jnp.where(lax.axis_index(axis) == source, block, jnp.zeros_like(block))
-    return lax.psum(block, axis)
+    return jnp.sum(lax.all_gather(block, axis), axis=0)
 
 
 def band_matrix():

time: 766 us -> 757 us (0.988)
  waiting for transfers between devices: 103 us -> 20.2 us
  blocking collectives: 224 us -> 297 us
    all_gather x0 -> x4, blocking collectives: none -> 93.6 us  [broadcast(): return jnp.sum(lax.all_gather(block, axis), axis=0)]
    psum x1 -> x0, waiting for transfers between devices: 82.3 us -> none  [broadcast(): return lax.psum(block, axis)]
    all_to_all x1, blocking collectives: 213 us -> 193 us  [shards(): lax.all_to_all(buffer, 'chan', split_axis=1, concat_axis=1, tiled=True)]
    unnamed x3 -> x2, waiting for transfers between devices: 20.2 us -> 20.2 us
    unnamed x10 -> x8, local copies, waits for them, and re-layouts: 42.2 us -> 42.2 us
  transfers between devices with their start and end apart: 2 -> 1, of which waited for: 2 -> 1; matrix products, arithmetic and copies ran while one was open for 0% -> 0% of each run, Pallas kernels for 0% -> 0%
where the time goes in v1:
time: 757 us; the launch traced here: 749 us
  blocking collectives  297 us (39%)
  local copies, waits for them, and re-layouts  191 us (25%)
  other arithmetic  141 us (19%)
  matrix products  63.9 us (8%)
  between operations  23.8 us (3%)
  waiting for transfers between devices  20.2 us (3%)
  loops' own time  11.3 us (1%)
    all_to_all x1, blocking collectives, shards(): lax.all_to_all(buffer, 'chan', split_axis=1, concat_axis=1, tiled=True)  193 us
    all_gather x4, blocking collectives, broadcast(): return jnp.sum(lax.all_gather(block, axis), axis=0)  93.6 us
    another operation x17, other arithmetic  78.3 us
    dot_general x16, matrix products, correlate_block(): jnp.dot(cross_rows, lag_table(first_lag, lag_count), preferred_element_ty...  59.6 us
    unnamed x8, local copies, waits for them, and re-layouts  42.2 us
    gather x3, local copies, waits for them, and re-layouts, gather_rows(): block_rows[chosen]  31.8 us
    reduce_sum x16, other arithmetic, correlate_block(): return terms.reshape(-1, windows, 3, lag_count).sum(axis=1)  26.3 us
    reshape x2, local copies, waits for them, and re-layouts, shards(): jnp.transpose(pieces, (1, 2, 3, 0, 4))  26.1 us
  transfers between devices with their start and end apart: 1, of which 1 were waited for; matrix products, arithmetic and copies ran while one was open for 0% of the time, Pallas kernels for 0%

profile of v1, /device:TPU:0, one launch (start us, length us, event | category | flops | bytes accessed | tf_op | source)
XLA Modules:
  0.0 748.6 jit_solution(2772717627859626809)
XLA Ops:
  16.8 3.2 fusion.45
  20.0 4.3 fusion.30
  29.4 25.3 %all_gather.16 = bf16[16,4,2,1024]{3,1,2,0:T(4,128)(2,1)S(1)} all-gather(bf16[1,4,2,1024]{3,1,2,0:T(4,128)(2,1)S(1)} %copy.75), channel_id=1, replica_groups=mesh['chan'=16,'win'=8] {'chan'}, dimensions={0}, use_global_device_ids=true | all-gather | bytes 278528 | tf_op jit(solution)/shard_map/all_gather | solution.py:20
  54.8 23.2 %all_gather.17 = bf16[16,4,2,1024]{3,1,2,0:T(4,128)(2,1)S(1)} all-gather(bf16[1,4,2,1024]{3,1,2,0:T(4,128)(2,1)S(1)} %copy.76), channel_id=1, replica_groups=mesh['chan'=16,'win'=8] {'chan'}, dimensions={0}, use_global_device_ids=true | all-gather | bytes 278528 | tf_op jit(solution)/shard_map/all_gather | solution.py:20
  78.2 21.6 %all_gather.18 = bf16[16,4,2,1024]{3,1,2,0:T(4,128)(2,1)S(1)} all-gather(bf16[1,4,2,1024]{3,1,2,0:T(4,128)(2,1)S(1)} %copy.77), channel_id=1, replica_groups=mesh['chan'=16,'win'=8] {'chan'}, dimensions={0}, use_global_device_ids=true | all-gather | bytes 278528 | tf_op jit(solution)/shard_map/all_gather | solution.py:20
  99.9 23.6 %all_gather.19 = bf16[16,4,2,1024]{3,1,2,0:T(4,128)(2,1)S(1)} all-gather(bf16[1,4,2,1024]{3,1,2,0:T(4,128)(2,1)S(1)} %copy.78), channel_id=1, replica_groups=mesh['chan'=16,'win'=8] {'chan'}, dimensions={0}, use_global_device_ids=true | all-gather | bytes 278528 | tf_op jit(solution)/shard_map/all_gather | solution.py:20
  123.6 2.8 add_convert_fusion
  126.5 1.9 add.109
  128.3 1.8 sub.32
  130.2 3.4 pad_maximum_fusion
  133.6 226.1 %while.12 = (s32[]{:T(128)}, f32[16,192,3,256]{3,1,2,0:T(8,128)}, s32[16]{0:T(128)S(1)}, bf16[768,2048]{1,0:T(8,128)(2,1)}, s32[]{:T(128)}, /*index=5*/s32[1]{0:T(128)}) while((s32[]{:T(128)}, f32[16,192,3,256]{3,1,2,0:T(8,128)}, s32[16]{0:T(128)S(1)}, bf16[768,2048]{1,0:T(8,128)(2,1)}, s32[]{:T(128)}, /*index=5*/s32[1]{0:T(128)}) %tuple.55), condition=%wide.region_6.7_spmd, body=%wide.region_4.6_spmd.sunk | while | flops 1626916352 | bytes 25373280 | solution.py:122
  134.8 4.7 fusion.55
  139.6 3.7 multiply_bitcast_fusion.2
  145.2 1.6 maximum_reduce_fusion.2
  148.9 4.7 fusion.55
  153.7 3.7 multiply_bitcast_fusion.2
  159.3 1.6 maximum_reduce_fusion.2
  163.0 4.7 fusion.55
  167.8 3.7 multiply_bitcast_fusion.2
  173.4 1.6 maximum_reduce_fusion.2
  177.2 4.7 fusion.55
  181.9 3.7 multiply_bitcast_fusion.2
  187.5 1.6 maximum_reduce_fusion.2
  191.3 4.7 fusion.55
  196.0 3.7 multiply_bitcast_fusion.2
  201.7 1.6 maximum_reduce_fusion.2
  205.4 4.7 fusion.55
  210.2 3.7 multiply_bitcast_fusion.2
  215.8 1.6 maximum_reduce_fusion.2
  219.5 4.7 fusion.55
  224.3 3.7 multiply_bitcast_fusion.2
  233.6 4.7 fusion.55
  238.4 3.7 multiply_bitcast_fusion.2
  247.7 4.7 fusion.55
  252.5 3.7 multiply_bitcast_fusion.2
  261.9 4.7 fusion.55
  266.6 3.7 multiply_bitcast_fusion.2
  276.0 4.7 fusion.55
  280.7 3.7 multiply_bitcast_fusion.2
  290.1 4.7 fusion.55
  294.8 3.7 multiply_bitcast_fusion.2
  304.2 4.7 fusion.55
  309.0 3.7 multiply_bitcast_fusion.2
  318.3 4.7 fusion.55
  323.1 3.7 multiply_bitcast_fusion.2
  328.7 1.6 maximum_reduce_fusion.2
  332.4 4.7 fusion.55
  337.2 3.7 multiply_bitcast_fusion.2
  346.6 4.7 fusion.55
  351.3 3.7 multiply_bitcast_fusion.2
  359.7 13.8 %copy.118 = f32[16,4,48,3,256]{4,0,2,3,1:T(8,128)} copy(f32[16,4,48,3,256]{4,2,1,3,0:T(8,128)} %bitcast.102) | data formatting | bytes 18874368 | tf_op jit(solution)/shard_map/reshape | solution.py:123
  373.5 11.3 %reshape.178 = f32[4,48,3,4096]{3,1,2,0:T(8,128)} reshape(f32[4,48,3,16,256]{4,3,1,2,0:T(8,128)} %bitcast.100) | data formatting | bytes 18874368 | tf_op jit(solution)/shard_map/reshape | solution.py:124
  384.9 14.8 %copy.82 = f32[4,48,3,4096]{3,2,1,0:T(4,128)} copy(f32[4,48,3,4096]{3,1,2,0:T(8,128)} %reshape.178) | data formatting | bytes 18874368 | tf_op jit(solution)/shard_map/reshape | solution.py:124
  400.1 31.5 %gather_fusion = f32[384,3,4096]{2,1,0:T(4,128)} fusion(f32[4,48,3,4096]{3,2,1,0:T(4,128)} %copy.82, s32[384]{0:T(512)S(1)} %reshape.184), kind=kCustom, calls=%fused_computation | custom fusion | bytes 37751808 | tf_op jit(solution)/shard_map/vmap()/gather | solution.py:82
  431.7 12.7 %copy_multiply_fusion = f32[4,16,6,3,4096]{4,2,1,0,3:T(8,128)S(1)} fusion(f32[4,16,6,3,4096]{4,3,2,1,0:T(4,128)} %bitcast.99, f32[4,16,6]{2,1,0:T(8,128)S(1)} %reshape.183), kind=kLoop, calls=%fused_computation.30 | loop fusion | flops 4718592 | bytes 37750272 | tf_op jit(solution)/shard_map/mul | solution.py:83
  444.4 17.2 %copy.85 = f32[4,16,6,3,4096]{4,0,3,2,1:T(4,128)} copy(f32[4,16,6,3,4096]{4,2,1,0,3:T(8,128)S(1)} %copy_multiply_fusion) | data formatting | bytes 37748736 | tf_op jit(solution)/shard_map/mul | solution.py:83
  461.6 192.7 %all_to_all.10 = f32[4,16,6,3,4096]{4,0,3,2,1:T(4,128)} all-to-all(f32[4,16,6,3,4096]{4,0,3,2,1:T(4,128)} %copy.85), channel_id=1, replica_groups=mesh['chan'=16,'win'=8] {'chan'}, dimensions={1} | all-to-all | bytes 37748736 | tf_op jit(solution)/shard_map/all_to_all | solution.py:128
  654.3 10.5 %reduce_sum.96 = f32[4,6,3,4096]{3,0,2,1:T(4,128)S(1)} reduce(f32[4,16,6,3,4096]{4,0,3,2,1:T(4,128)} %all_to_all.10, f32[]{:T(128)} %constant.119.clone.1), dimensions={1}, to_apply=%region_7.8 | reduce | flops 4423680 | bytes 20054020 | tf_op jit(solution)/shard_map/reduce_sum | solution.py:94
  665.1 16.9 %copy.91 = f32[4,2,3,4096]{1,0,2,3:T(4,128)} copy(f32[4,2,3,4096]{3,0,2,1:T(4,128)S(1)} %reduce_sum.98) | data formatting | bytes 786432
  682.0 18.1 %reshape.197 = f32[4096,24]{1,0:T(8,128)} reshape(f32[4096,3,4,2]{3,2,1,0:T(4,128)} %bitcast.98) | data formatting | bytes 786432
  700.2 11.1 %all_to_all.11 = f32[4,16,6]{2,0,1:T(4,128)S(1)} all-to-all(f32[4,16,6]{2,0,1:T(4,128)S(1)} %copy.89), channel_id=1, replica_groups=mesh['chan'=16,'win'=8] {'chan'}, dimensions={1} | all-to-all | bytes 3072 | tf_op jit(solution)/shard_map/all_to_all | solution.py:129
  711.5 20.2 %reduce-scatter.4.cloned.1.call-done = f32[512,24]{1,0:T(8,128)} async-done(((f32[4096,24]{1,0:T(8,128)}), f32[512,24]{1,0:T(8,128)}) %reduce-scatter.4.cloned.1.call-update) | async-done | bytes 49168
  731.7 2.5 reshape.198
  734.2 1.9 fusion.44
  (222 shorter events, 80.5 us)
Async XLA Ops:
  6.5 725.2 %reduce-scatter.4.cloned.1.call-start = ((), (), s32[]{:S(2)}) async-start(), calls=%async_computation.3 | async-start | bytes 2359296
  128.3 1.9 copy-start
Sparse Core Ops, SparseCore 0:
  700.3 31.3 reduce-scatter.3
